TPU v7x, 128 devices: a whole 4x4x4 slice. The times are simulated.
128 devices in a mesh: row: 8 (over z, core), col: 16 (over y, x).
Axes of the slice: x: 4, y: 4, z: 4, core: 2. Of those that a mesh axis runs over, the one named last changes fastest.
Arguments:
- front_diag: float32 [1024, 1024], replicated, may hold values from -4 to 16, as said below
- panel_rows: float32 [16384, 1024], P(('row', 'col')), may hold values from -1.2 to 1.2
- trailing: float32 [16384, 16384], P('row', 'col'), may hold values from -6 to 6
- pattern: int32 [64, 64], P('row', 'col'), may hold values 0 or 1
Outputs:
- diag_factor: float32 [1024, 1024], replicated
- panel_factor: float32 [16384, 1024], P(('row', 'col'))
- schur: float32 [16384, 16384], P('row', 'col')
Inputs may be any that keep to these rules, and one draw needn't show every extreme that they name: front_diag is symmetric and positive definite, with smallest eigenvalue at least 0.5.
All inputs are finite; a program needn't handle non-finite values. No bound on the sum of `pattern` on one device may be relied on, other than what follows from the above.
Results may differ from a plain program's by a relative error of at most 0.0003.
Values sent between devices are 32-bit elements; how exact they have to be, the bound alone decides.
A program may use at most 128 MiB of HBM per device.

v0:
```python
import jax
import jax.numpy as jnp
from jax import lax
from jax.sharding import PartitionSpec as P

BLOCK = 256


def spread(block, axis, holder):
    block = jnp.where(lax.axis_index(axis) == holder, block, jnp.zeros_like(block))
    return lax.psum(block, axis)


def column_rows(row_part, col_rows):
    ratio = lax.axis_size("col") // lax.axis_size("row")
    offset = lax.axis_index("col") % ratio * col_rows
    return lax.dynamic_slice_in_dim(row_part, offset, col_rows, 0)


def local(front_diag, panel_rows, trailing, pattern):
    diag_factor = jnp.linalg.cholesky(front_diag)
    panel_factor = jax.scipy.linalg.solve_triangular(diag_factor, panel_rows.T, lower=True).T
    local_rows = trailing.shape[0]
    col_rows = trailing.shape[1]
    ratio = lax.axis_size("col") // lax.axis_size("row")
    root_row = lax.axis_index("col") // ratio
    row_part = lax.all_gather(panel_factor, "col", axis=0, tiled=True)
    piece = column_rows(row_part, col_rows)
    col_part = spread(piece, "row", root_row)
    update = jnp.dot(row_part, col_part.T, precision=lax.Precision.HIGHEST)
    row_blocks = local_rows // BLOCK
    col_blocks = col_rows // BLOCK
    row_index = lax.axis_index("row") * row_blocks + jnp.arange(row_blocks)
    col_index = lax.axis_index("col") * col_blocks + jnp.arange(col_blocks)
    lower = (row_index[:, None] >= col_index[None, :]).astype(jnp.float32)
    keep = pattern.astype(jnp.float32) * lower
    masked = update.reshape(row_blocks, BLOCK, col_blocks, BLOCK) * keep[:, None, :, None]
    schur = trailing - masked.reshape(local_rows, col_rows)
    return (diag_factor, panel_factor, schur)


def solution(mesh):
    return jax.shard_map(
        local,
        mesh=mesh,
        in_specs=(P(), P(("row", "col"), None), P("row", "col"), P("row", "col")),
        out_specs=(P(), P(("row", "col"), None), P("row", "col")),
        check_vma=False,
    )
```

profile of v0, /device:TPU:0, one launch (start us, length us, event | category | flops | bytes accessed | tf_op | source)
XLA Modules:
  0.0 537.7 jit_solution(12177218288238149050)
XLA Ops:
  7.2 5.3 copy.7
  19.0 11.7 %cholesky.223 = f32[128,128]{1,0:T(8,128)S(1)} custom-call(f32[128,128]{1,0:T(8,128)S(1)} %cholesky.580), custom_call_target="Cholesky" | custom-call | tf_op jit(solution)/shard_map/jit(cholesky)/cholesky | solution.py:21
  30.8 9.8 %custom-call.63 = f32[1,128,128]{1,2,0:T(8,128)S(1)} custom-call(f32[1,128,128]{2,1,0:T(8,128)S(1)} %get-tuple-element.61), custom_call_target="InvertDiagBlocksLowerTriangular" | custom-call | tf_op jit(solution)/shard_map/jit(cholesky)/cholesky | solution.py:21
  47.0 11.9 %cholesky.244 = f32[128,128]{1,0:T(8,128)S(1)} custom-call(f32[128,128]{1,0:T(8,128)S(1)} %cholesky.584), custom_call_target="Cholesky" | custom-call | tf_op jit(solution)/shard_map/jit(cholesky)/cholesky | solution.py:21
  59.5 9.8 %custom-call.64 = f32[1,128,128]{1,2,0:T(8,128)S(1)} custom-call(f32[1,128,128]{2,1,0:T(8,128)S(1)} %get-tuple-element.58), custom_call_target="InvertDiagBlocksLowerTriangular" | custom-call | tf_op jit(solution)/shard_map/jit(cholesky)/cholesky | solution.py:21
  72.7 11.7 %cholesky.468 = f32[128,128]{1,0:T(8,128)S(1)} custom-call(f32[128,128]{1,0:T(8,128)S(1)} %cholesky.589), custom_call_target="Cholesky" | custom-call | tf_op jit(solution)/shard_map/jit(cholesky)/cholesky | solution.py:21
  85.7 9.8 %custom-call.65 = f32[1,128,128]{1,2,0:T(8,128)S(1)} custom-call(f32[1,128,128]{2,1,0:T(8,128)S(1)} %get-tuple-element.55), custom_call_target="InvertDiagBlocksLowerTriangular" | custom-call | tf_op jit(solution)/shard_map/jit(cholesky)/cholesky | solution.py:21
  99.0 11.9 %cholesky.487 = f32[128,128]{1,0:T(8,128)S(1)} custom-call(f32[128,128]{1,0:T(8,128)S(1)} %cholesky.594), custom_call_target="Cholesky" | custom-call | tf_op jit(solution)/shard_map/jit(cholesky)/cholesky | solution.py:21
  112.2 9.8 %custom-call.66 = f32[1,128,128]{1,2,0:T(8,128)S(1)} custom-call(f32[1,128,128]{2,1,0:T(8,128)S(1)} %get-tuple-element.52), custom_call_target="InvertDiagBlocksLowerTriangular" | custom-call | tf_op jit(solution)/shard_map/jit(cholesky)/cholesky | solution.py:21
  125.4 11.7 %cholesky.506 = f32[128,128]{1,0:T(8,128)S(1)} custom-call(f32[128,128]{1,0:T(8,128)S(1)} %cholesky.599), custom_call_target="Cholesky" | custom-call | tf_op jit(solution)/shard_map/jit(cholesky)/cholesky | solution.py:21
  138.5 10.2 %custom-call.67 = f32[1,128,128]{1,2,0:T(8,128)S(1)} custom-call(f32[1,128,128]{2,1,0:T(8,128)S(1)} %get-tuple-element.49), custom_call_target="InvertDiagBlocksLowerTriangular" | custom-call | tf_op jit(solution)/shard_map/jit(cholesky)/cholesky | solution.py:21
  152.0 11.7 %cholesky.526 = f32[128,128]{1,0:T(8,128)S(1)} custom-call(f32[128,128]{1,0:T(8,128)S(1)} %cholesky.604), custom_call_target="Cholesky" | custom-call | tf_op jit(solution)/shard_map/jit(cholesky)/cholesky | solution.py:21
  165.0 9.8 %custom-call.68 = f32[1,128,128]{1,2,0:T(8,128)S(1)} custom-call(f32[1,128,128]{2,1,0:T(8,128)S(1)} %get-tuple-element.46), custom_call_target="InvertDiagBlocksLowerTriangular" | custom-call | tf_op jit(solution)/shard_map/jit(cholesky)/cholesky | solution.py:21
  177.9 11.9 %cholesky.546 = f32[128,128]{1,0:T(8,128)S(1)} custom-call(f32[128,128]{1,0:T(8,128)S(1)} %cholesky.609), custom_call_target="Cholesky" | custom-call | tf_op jit(solution)/shard_map/jit(cholesky)/cholesky | solution.py:21
  191.0 9.8 %custom-call.69 = f32[1,128,128]{1,2,0:T(8,128)S(1)} custom-call(f32[1,128,128]{2,1,0:T(8,128)S(1)} %get-tuple-element.43), custom_call_target="InvertDiagBlocksLowerTriangular" | custom-call | tf_op jit(solution)/shard_map/jit(cholesky)/cholesky | solution.py:21
  203.4 11.7 %cholesky.564 = f32[128,128]{1,0:T(8,128)S(1)} custom-call(f32[128,128]{1,0:T(8,128)S(1)} %convolution_subtract_fusion.11), custom_call_target="Cholesky" | custom-call | tf_op jit(solution)/shard_map/jit(cholesky)/cholesky | solution.py:21
  222.0 6.8 %fusion.1 = (f32[1024,1024]{1,0:T(8,128)}, f32[1024,1024]{1,0:T(8,128)}) fusion(f32[1024,1024]{1,0:T(8,128)} %get-tuple-element.41, pred[]{:T(512)S(6)} %cholesky.579), kind=kLoop, calls=%fused_computation.8 | loop fusion | flops 4194304 | bytes 12582913 | tf_op jit(solution)/shard_map/jit(_solve_triangular)/triangular_solve | solution.py:22
  228.8 22.5 %while.1 = (s32[]{:T(128)}, f32[1024,1024]{1,0:T(8,128)}, s32[8,2]{0,1:T(2,128)S(1)}, f32[8,128,128]{2,1,0:T(8,128)S(1)}, s32[]{:T(128)}) while((s32[]{:T(128)}, f32[1024,1024]{1,0:T(8,128)}, s32[8,2]{0,1:T(2,128)S(1)}, f32[8,128,128]{2,1,0:T(8,128)S(1)}, s32[]{:T(128)}) %tuple.58), condition=%wide.while_cond, body=%wide.while_body.sunk | while | flops 2 | bytes 131189 | solution.py:22
  251.3 78.8 %custom-call.70 = f32[8,128,128]{1,2,0:T(8,128)S(1)} custom-call(f32[8,128,128]{2,1,0:T(8,128)S(1)} %get-tuple-element.10), custom_call_target="InvertDiagBlocksLowerTriangular" | custom-call | tf_op jit(solution)/shard_map/jit(_solve_triangular)/triangular_solve | solution.py:22
  344.9 73.2 %all-gather.2.cloned.1.call-done = f32[2048,1024]{1,0:T(8,128)} async-done(((f32[128,1024]{1,0:T(8,128)}), f32[2048,1024]{1,0:T(8,128)}) %all-gather.2.cloned.1.call-update) | async-done | bytes 8388624 | tf_op jit(solution)/shard_map/all_gather | solution.py:27
  418.1 5.0 dynamic-slice_select_fusion
  425.0 5.5 %copy.18 = f32[256,8,4,256]{3,1,2,0:T(8,128)} copy(f32[256,8,4,256]{3,2,1,0:T(4,128)S(1)} %bitcast.109) | data formatting | bytes 16777216
  430.5 65.2 %all-reduce.3.cloned.1.call-done = f32[1024,1024]{1,0:T(8,128)} async-done(((f32[1024,1024]{1,0:T(8,128)}), f32[1024,1024]{1,0:T(8,128)}) %all-reduce.3.cloned.1.call-update) | async-done | bytes 4194320 | tf_op jit(solution)/shard_map/psum | solution.py:11
  495.8 34.7 %multiply_subtract_fusion = f32[2048,1024]{1,0:T(8,128)} fusion(f32[2048,1024]{1,0:T(8,128)} %param.6, f32[2048,1024]{1,0:T(8,128)} %bitcast.108, f32[2048,1024]{1,0:T(8,128)} %all-gather.2.cloned.1.call-done, f32[1024,1024]{1,0:T(8,128)} %all-reduce.3.cloned.1.call-done), kind=kOutput, calls=%fused_computation.2 | convolution fusion | flops 25773998080 | bytes 37748736 | tf_op jit(solution)/shard_map/dot_general | solution.py:30
  (111 shorter events, 80.0 us)
Async XLA Ops:
  7.2 410.9 %all-gather.2.cloned.1.call-start = ((), (), s32[]{:S(2)}) async-start(), calls=%async_computation | async-start | bytes 8912896 | tf_op jit(solution)/shard_map/all_gather | solution.py:27
  17.0 2.0 copy-start
  222.0 108.2 %copy-start.2 = (f32[128,1024]{1,0:T(8,128)S(1)}, f32[128,1024]{1,0:T(8,128)}, u32[]{:S(2)}) copy-start(f32[128,1024]{1,0:T(8,128)} %param.5) | copy-start | bytes 1572868
  344.0 0.8 copy-start.1
  344.8 150.9 %all-reduce.3.cloned.1.call-start = ((), (), s32[]{:S(2)}) async-start(), calls=%async_computation.1 | async-start | bytes 8388608 | tf_op jit(solution)/shard_map/psum | solution.py:11
  423.1 0.7 copy-start.3
Sparse Core Ops, SparseCore 0:
  345.0 73.0 all-gather.1
  423.2 72.5 all-reduce.2
where the time goes:
time: 548 us; the launch traced here: 538 us
  other arithmetic  267 us (49%)
  waiting for transfers between devices  138 us (25%)
  matrix products  70.7 us (13%)
  local copies, waits for them, and re-layouts  41.1 us (8%)
  between operations  19.9 us (4%)
    another operation x30, other arithmetic, local(): diag_factor = jnp.linalg.cholesky(front_diag)  172 us
    another operation x3, other arithmetic, local(): jax.scipy.linalg.solve_triangular(diag_factor, panel_rows.T, lower=True)  85.7 us
    all_gather x1, waiting for transfers between devices, local(): row_part = lax.all_gather(panel_factor, 'col', axis=0, tiled=True)  73.2 us
    psum x1, waiting for transfers between devices, spread(): return lax.psum(block, axis)  65.2 us
    dot_general x1, matrix products, local(): update = jnp.dot(row_part, col_part.T, precision=lax.Precision.HIGHEST)  34.7 us
    another operation x14, matrix products, local(): diag_factor = jnp.linalg.cholesky(front_diag)  23 us
    another operation x24, local copies, waits for them, and re-layouts  22.4 us
    unnamed x17, local copies, waits for them, and re-layouts  14.3 us
  transfers between devices with their start and end apart: 2, of which 2 were waited for; matrix products, arithmetic and copies ran while one was open for 1% of the time, Pallas kernels for 0%

commit v1 on v0

--- a/solution.py
+++ b/solution.py
@@ -4,6 +4,11 @@
 from jax.sharding import PartitionSpec as P
 
 BLOCK = 256
+
+
+def exchange_gather(array, axis, dim):
+    stack = jnp.stack([array] * lax.axis_size(axis))
+    return jnp.concatenate(lax.all_to_all(stack, axis, 0, 0), axis=dim)
 
 
 def spread(block, axis, holder):
@@ -24,7 +29,7 @@
     col_rows = trailing.shape[1]
     ratio = lax.axis_size("col") // lax.axis_size("row")
     root_row = lax.axis_index("col") // ratio
-    row_part = lax.all_gather(panel_factor, "col", axis=0, tiled=True)
+    row_part = exchange_gather(panel_factor, "col", 0)
     piece = column_rows(row_part, col_rows)
     col_part = spread(piece, "row", root_row)
     update = jnp.dot(row_part, col_part.T, precision=lax.Precision.HIGHEST)

time: 548 us -> 651 us (1.19)
  waiting for transfers between devices: 138 us -> 188 us
  local copies, waits for them, and re-layouts: 41.1 us -> 77.7 us
  other arithmetic: 267 us -> 279 us
  starting transfers between devices: 0.08 us -> 7.22 us
    all_to_all x0 -> x1, waiting for transfers between devices: none -> 124 us  [exchange_gather(): return jnp.concatenate(lax.all_to_all(stack, axis, 0, 0), axis=dim)]
    all_gather x1 -> x0, waiting for transfers between devices: 73.2 us -> none  [local(): row_part = lax.all_gather(panel_factor, 'col', axis=0, tiled=True)]
    unnamed x17 -> x13, local copies, waits for them, and re-layouts: 14.3 us -> 37.5 us
    sub x0 -> x1, other arithmetic: none -> 11.7 us  [local(): schur = trailing - masked.reshape(local_rows, col_rows)]
    mul x1, local copies, waits for them, and re-layouts: 1.15 us -> 10.7 us  [local(): update.reshape(row_blocks, BLOCK, col_blocks, BLOCK)]
    all_to_all x0 -> x1, starting transfers between devices: none -> 7.17 us  [exchange_gather(): return jnp.concatenate(lax.all_to_all(stack, axis, 0, 0), axis=dim)]
    another operation x24 -> x25, local copies, waits for them, and re-layouts: 22.4 us -> 26.8 us
where the time goes in v1:
time: 651 us; the launch traced here: 641 us
  other arithmetic  279 us (43%)
  waiting for transfers between devices  188 us (29%)
  local copies, waits for them, and re-layouts  77.7 us (12%)
  matrix products  68.6 us (11%)
  between operations  19.8 us (3%)
  starting transfers between devices  7.22 us (1%)
    another operation x30, other arithmetic, local(): diag_factor = jnp.linalg.cholesky(front_diag)  172 us
    all_to_all x1, waiting for transfers between devices, exchange_gather(): return jnp.concatenate(lax.all_to_all(stack, axis, 0, 0), axis=dim)  124 us
    another operation x3, other arithmetic, local(): jax.scipy.linalg.solve_triangular(diag_factor, panel_rows.T, lower=True)  85.7 us
    psum x1, waiting for transfers between devices, spread(): return lax.psum(block, axis)  64 us
    unnamed x13, local copies, waits for them, and re-layouts  37.5 us
    dot_general x1, matrix products, local(): update = jnp.dot(row_part, col_part.T, precision=lax.Precision.HIGHEST)  32.5 us
    another operation x14, matrix products, local(): diag_factor = jnp.linalg.cholesky(front_diag)  23 us
    another operation x24, local copies, waits for them, and re-layouts  22.4 us
  transfers between devices with their start and end apart: 2, of which 2 were waited for; matrix products, arithmetic and copies ran while one was open for 1% of the time, Pallas kernels for 0%

profile of v1, /device:TPU:0, one launch (start us, length us, event | category | flops | bytes accessed | tf_op | source)
XLA Modules:
  0.0 640.5 jit_solution(1181591148166487707)
XLA Ops:
  19.0 11.7 %cholesky.223 = f32[128,128]{1,0:T(8,128)S(1)} custom-call(f32[128,128]{1,0:T(8,128)S(1)} %cholesky.580), custom_call_target="Cholesky" | custom-call | tf_op jit(solution)/shard_map/jit(cholesky)/cholesky | solution.py:26
  30.7 9.8 %custom-call.63 = f32[1,128,128]{1,2,0:T(8,128)S(1)} custom-call(f32[1,128,128]{2,1,0:T(8,128)S(1)} %get-tuple-element.75), custom_call_target="InvertDiagBlocksLowerTriangular" | custom-call | tf_op jit(solution)/shard_map/jit(cholesky)/cholesky | solution.py:26
  47.0 11.9 %cholesky.244 = f32[128,128]{1,0:T(8,128)S(1)} custom-call(f32[128,128]{1,0:T(8,128)S(1)} %cholesky.584), custom_call_target="Cholesky" | custom-call | tf_op jit(solution)/shard_map/jit(cholesky)/cholesky | solution.py:26
  59.5 9.8 %custom-call.64 = f32[1,128,128]{1,2,0:T(8,128)S(1)} custom-call(f32[1,128,128]{2,1,0:T(8,128)S(1)} %get-tuple-element.72), custom_call_target="InvertDiagBlocksLowerTriangular" | custom-call | tf_op jit(solution)/shard_map/jit(cholesky)/cholesky | solution.py:26
  72.6 11.7 %cholesky.468 = f32[128,128]{1,0:T(8,128)S(1)} custom-call(f32[128,128]{1,0:T(8,128)S(1)} %cholesky.589), custom_call_target="Cholesky" | custom-call | tf_op jit(solution)/shard_map/jit(cholesky)/cholesky | solution.py:26
  85.6 9.8 %custom-call.65 = f32[1,128,128]{1,2,0:T(8,128)S(1)} custom-call(f32[1,128,128]{2,1,0:T(8,128)S(1)} %get-tuple-element.69), custom_call_target="InvertDiagBlocksLowerTriangular" | custom-call | tf_op jit(solution)/shard_map/jit(cholesky)/cholesky | solution.py:26
  98.9 11.9 %cholesky.487 = f32[128,128]{1,0:T(8,128)S(1)} custom-call(f32[128,128]{1,0:T(8,128)S(1)} %cholesky.594), custom_call_target="Cholesky" | custom-call | tf_op jit(solution)/shard_map/jit(cholesky)/cholesky | solution.py:26
  112.1 9.8 %custom-call.66 = f32[1,128,128]{1,2,0:T(8,128)S(1)} custom-call(f32[1,128,128]{2,1,0:T(8,128)S(1)} %get-tuple-element.66), custom_call_target="InvertDiagBlocksLowerTriangular" | custom-call | tf_op jit(solution)/shard_map/jit(cholesky)/cholesky | solution.py:26
  125.4 11.7 %cholesky.506 = f32[128,128]{1,0:T(8,128)S(1)} custom-call(f32[128,128]{1,0:T(8,128)S(1)} %cholesky.599), custom_call_target="Cholesky" | custom-call | tf_op jit(solution)/shard_map/jit(cholesky)/cholesky | solution.py:26
  138.4 10.2 %custom-call.67 = f32[1,128,128]{1,2,0:T(8,128)S(1)} custom-call(f32[1,128,128]{2,1,0:T(8,128)S(1)} %get-tuple-element.63), custom_call_target="InvertDiagBlocksLowerTriangular" | custom-call | tf_op jit(solution)/shard_map/jit(cholesky)/cholesky | solution.py:26
  152.0 11.7 %cholesky.526 = f32[128,128]{1,0:T(8,128)S(1)} custom-call(f32[128,128]{1,0:T(8,128)S(1)} %cholesky.604), custom_call_target="Cholesky" | custom-call | tf_op jit(solution)/shard_map/jit(cholesky)/cholesky | solution.py:26
  165.0 9.8 %custom-call.68 = f32[1,128,128]{1,2,0:T(8,128)S(1)} custom-call(f32[1,128,128]{2,1,0:T(8,128)S(1)} %get-tuple-element.60), custom_call_target="InvertDiagBlocksLowerTriangular" | custom-call | tf_op jit(solution)/shard_map/jit(cholesky)/cholesky | solution.py:26
  177.8 11.9 %cholesky.546 = f32[128,128]{1,0:T(8,128)S(1)} custom-call(f32[128,128]{1,0:T(8,128)S(1)} %cholesky.609), custom_call_target="Cholesky" | custom-call | tf_op jit(solution)/shard_map/jit(cholesky)/cholesky | solution.py:26
  191.0 9.8 %custom-call.69 = f32[1,128,128]{1,2,0:T(8,128)S(1)} custom-call(f32[1,128,128]{2,1,0:T(8,128)S(1)} %get-tuple-element.57), custom_call_target="InvertDiagBlocksLowerTriangular" | custom-call | tf_op jit(solution)/shard_map/jit(cholesky)/cholesky | solution.py:26
  203.4 11.7 %cholesky.564 = f32[128,128]{1,0:T(8,128)S(1)} custom-call(f32[128,128]{1,0:T(8,128)S(1)} %convolution_subtract_fusion.11), custom_call_target="Cholesky" | custom-call | tf_op jit(solution)/shard_map/jit(cholesky)/cholesky | solution.py:26
  228.8 22.5 %while.1 = (s32[]{:T(128)}, f32[1024,1024]{1,0:T(8,128)}, s32[8,2]{0,1:T(2,128)S(1)}, f32[8,128,128]{2,1,0:T(8,128)S(1)}, s32[]{:T(128)}) while((s32[]{:T(128)}, f32[1024,1024]{1,0:T(8,128)}, s32[8,2]{0,1:T(2,128)S(1)}, f32[8,128,128]{2,1,0:T(8,128)S(1)}, s32[]{:T(128)}) %tuple.64), condition=%wide.while_cond, body=%wide.while_body.sunk | while | flops 2 | bytes 131189 | solution.py:27
  251.3 78.8 %custom-call.70 = f32[8,128,128]{1,2,0:T(8,128)S(1)} custom-call(f32[8,128,128]{2,1,0:T(8,128)S(1)} %get-tuple-element.10), custom_call_target="InvertDiagBlocksLowerTriangular" | custom-call | tf_op jit(solution)/shard_map/jit(_solve_triangular)/triangular_solve | solution.py:27
  355.3 123.9 %all-to-all-done = f32[16,128,1024]{2,1,0:T(8,128)} async-done(((f32[16,128,1024]{2,1,0:T(8,128)}), f32[16,128,1024]{2,1,0:T(8,128)}, u32[]{:S(2)}, u32[]{:S(2)}) %all-to-all-start) | async-done | bytes 8388640 | tf_op jit(solution)/shard_map/all_to_all | solution.py:11
  485.1 9.4 %copy.15 = f32[2048,1024]{0,1:T(8,128)} copy(f32[2048,1024]{1,0:T(8,128)} %param.6) | data formatting | bytes 16777216 | tf_op args[2]
  494.4 64.0 %all-reduce.3.cloned.1.call-done = f32[4,256,1024]{2,1,0:T(8,128)} async-done(((f32[4,256,1024]{2,1,0:T(8,128)}), f32[4,256,1024]{2,1,0:T(8,128)}) %all-reduce.3.cloned.1.call-update) | async-done | bytes 4194320 | tf_op jit(solution)/shard_map/psum | solution.py:16
  558.4 32.5 %broadcast_multiply_fusion = f32[8,256,4,256]{3,1,2,0:T(8,128)} fusion(f32[8,4]{1,0:T(8,128)S(1)} %copy.13, f32[8,256,1024,1]{2,1,3,0:T(8,128)} %bitcast.27, f32[4,256,1024]{2,1,0:T(8,128)} %all-reduce.3.cloned.1.call-done), kind=kOutput, calls=%fused_computation.6 | convolution fusion | flops 25771900928 | bytes 20971648 | tf_op jit(solution)/shard_map/dot_general | solution.py:35
  590.9 10.7 %copy.14 = f32[8,256,4,256]{1,0,3,2:T(8,128)} copy(f32[8,256,4,256]{3,1,2,0:T(8,128)} %broadcast_multiply_fusion) | data formatting | bytes 16777216 | tf_op jit(solution)/shard_map/mul | solution.py:42
  601.5 10.7 %copy.19 = f32[128,8,8,256]{3,1,2,0:T(8,128)} copy(f32[128,8,8,256]{3,2,1,0:T(8,128)} %bitcast.122) | data formatting | bytes 16777216
  612.2 11.7 %sub.8 = f32[2048,1024]{0,1:T(8,128)} subtract(f32[2048,1024]{0,1:T(8,128)} %copy.15, f32[2048,1024]{0,1:T(8,128)} %bitcast.121) | non-fusion elementwise | flops 2097152 | bytes 25165824 | tf_op jit(solution)/shard_map/sub | solution.py:43
  (101 shorter events, 115.7 us)
Async XLA Ops:
  17.0 2.0 copy-start
  221.9 108.2 %copy-start.2 = (f32[128,1024]{1,0:T(8,128)S(1)}, f32[128,1024]{1,0:T(8,128)}, u32[]{:S(2)}) copy-start(f32[128,1024]{1,0:T(8,128)} %param.5) | copy-start | bytes 1572868
  343.5 4.5 copy-start.1
  348.0 131.2 %all-to-all-start = ((f32[16,128,1024]{2,1,0:T(8,128)}), f32[16,128,1024]{2,1,0:T(8,128)}, u32[]{:S(2)}, u32[]{:S(2)}) async-start(f32[16,128,1024]{2,1,0:T(8,128)} %stack.2), calls=%async_computation | async-start | bytes 16777216 | tf_op jit(solution)/shard_map/all_to_all | solution.py:11
  355.2 203.1 %all-reduce.3.cloned.1.call-start = ((), (), s32[]{:S(2)}) async-start(), calls=%async_computation.1 | async-start | bytes 8388608 | tf_op jit(solution)/shard_map/psum | solution.py:16
  484.2 0.7 copy-start.3
Sparse Core Ops, SparseCore 0:
  484.4 73.9 all-reduce.2
